TPU v7x, 32 devices: a whole 2x2x4 slice. The times are simulated.
32 devices in a mesh: view: 8 (over z, core), strip: 2 (over x), orbit: 2 (over y).
Axes of the slice: x: 2, y: 2, z: 4, core: 2. Of those that a mesh axis runs over, the one named last changes fastest.
Arguments:
- features: bfloat16 [16, 8, 128, 256], P(('orbit', 'view'), 'strip'), parts along dimension 0, may hold values from -6 to 6
- cotangent: bfloat16 [16, 8, 128, 256], P(('orbit', 'view'), 'strip'), parts along dimension 0, may hold values from -6 to 6
- conv_first: bfloat16 [3, 3, 256, 256], replicated, may hold values from -0.125 to 0.125
- conv_second: bfloat16 [3, 3, 256, 256], replicated, may hold values from -0.125 to 0.125
- w_query: bfloat16 [256, 256], replicated, may hold values from -6 to 6
- w_key: bfloat16 [256, 256], replicated, may hold values from -6 to 6
- w_value: bfloat16 [256, 256], replicated, may hold values from -0.375 to 0.375
- w_out: bfloat16 [256, 256], replicated, may hold values from -0.375 to 0.375
Outputs:
- grad_features: bfloat16 [16, 8, 128, 256], P(('orbit', 'view'), 'strip'), parts along dimension 0
- conv_grads: float32 [4, 2304, 256], P('orbit', 'view'), parts along dimension 0
- attn_grads: float32 [8, 256, 256], P('orbit', 'view'), parts along dimension 0
There are 2 independent parts, one for each index of `orbit`. A program takes and returns all parts, laid end to end along the dimension named above; an argument that names none is the same for every part. Nothing has to cross between parts.
All inputs are finite; a program needn't handle non-finite values.
Results may differ from a plain program's by a relative error of at most 0.017.
Values may be sent and summed in bfloat16 or wider, within the bound.
A program may use at most 64 MiB of HBM per device.

v0:
```python
import jax
import jax.numpy as jnp
from jax import lax
from jax.sharding import PartitionSpec as P


def extended(block, sides, width):
    for axis, dim in sides:
        count = lax.axis_size(axis)
        forward = [(i, i + 1) for i in range(count - 1)]
        backward = [(target, source) for source, target in forward]
        low = lax.ppermute(
            lax.slice_in_dim(block, block.shape[dim] - width, None, axis=dim), axis, forward
        )
        high = lax.ppermute(lax.slice_in_dim(block, 0, width, axis=dim), axis, backward)
        block = jnp.concatenate([low, block, high], axis=dim)
    return block


def rounded(array):
    return lax.optimization_barrier(array.astype(jnp.bfloat16))


def silu_slope(value):
    sigma = jax.nn.sigmoid(value)
    return sigma * (1.0 + value * (1.0 - sigma))


def with_rims(array):
    padded = extended(array, (("strip", 1),), 1)
    return jnp.pad(padded, ((0, 0), (0, 0), (1, 1), (0, 0)))


def flipped(kernel):
    return jnp.transpose(kernel[::-1, ::-1], (0, 1, 3, 2))


def convolve(padded, kernel):
    lead = padded.shape[0]
    rows = padded.shape[1] - 2
    cols = padded.shape[2] - 2
    chan = padded.shape[3]
    total = jnp.zeros((lead * rows * cols, kernel.shape[3]), jnp.float32)
    for shift_row in range(3):
        for shift_col in range(3):
            piece = padded[
                :, shift_row : shift_row + rows, shift_col : shift_col + cols, :
            ].reshape(-1, chan)
            total = total + jnp.dot(
                piece, kernel[shift_row, shift_col], preferred_element_type=jnp.float32
            )
    return total.reshape(lead, rows, cols, -1)


def kernel_grad(padded, upstream):
    rows = padded.shape[1] - 2
    cols = padded.shape[2] - 2
    chan = padded.shape[3]
    flat_up = upstream.reshape(-1, upstream.shape[3])
    pieces = []
    for shift_row in range(3):
        for shift_col in range(3):
            piece = padded[
                :, shift_row : shift_row + rows, shift_col : shift_col + cols, :
            ].reshape(-1, chan)
            pieces.append(
                lax.dot_general(
                    piece, flat_up, (((0,), (0,)), ((), ())), preferred_element_type=jnp.float32
                )
            )
    return jnp.stack(pieces).reshape(9 * chan, -1)


def attend(query, key, value, grad_mixed):
    chan = query.shape[-1]
    scale = chan ** (-0.5)
    scores = jnp.einsum("amc,bmc->mab", query, key, preferred_element_type=jnp.float32) * scale
    top = jnp.max(scores, axis=-1, keepdims=True)
    expo = jnp.exp(scores - top)
    prob_f = expo / jnp.sum(expo, axis=-1, keepdims=True)
    prob = prob_f.astype(jnp.bfloat16)
    mixed = jnp.einsum("mab,bmc->amc", prob, value, preferred_element_type=jnp.float32).astype(
        jnp.bfloat16
    )
    grad_prob = jnp.einsum("amc,bmc->mab", grad_mixed, value, preferred_element_type=jnp.float32)
    grad_value = jnp.einsum(
        "mab,amc->bmc", prob, grad_mixed, preferred_element_type=jnp.float32
    ).astype(jnp.bfloat16)
    inner = jnp.sum(prob_f * grad_prob, axis=-1, keepdims=True)
    grad_score = (prob_f * (grad_prob - inner) * scale).astype(jnp.bfloat16)
    grad_query = jnp.einsum(
        "mab,bmc->amc", grad_score, key, preferred_element_type=jnp.float32
    ).astype(jnp.bfloat16)
    grad_key = jnp.einsum(
        "mab,amc->bmc", grad_score, query, preferred_element_type=jnp.float32
    ).astype(jnp.bfloat16)
    return (mixed, grad_query, grad_key, grad_value)


def project(flat, weight):
    return jnp.dot(flat, weight, preferred_element_type=jnp.float32).astype(jnp.bfloat16)


def project_back(flat, weight):
    return lax.dot_general(
        flat, weight, (((1,), (1,)), ((), ())), preferred_element_type=jnp.float32
    )


def outer_sum(left, right):
    return lax.dot_general(
        left, right, (((0,), (0,)), ((), ())), preferred_element_type=jnp.float32
    )


def body(features, cotangent, conv_first, conv_second, w_query, w_key, w_value, w_out):
    chan = features.shape[3]
    pixels = features.shape[1] * features.shape[2]
    views = lax.axis_size("view")
    share = pixels // views
    inputs_f = features.astype(jnp.float32)
    act_first = jax.nn.silu(inputs_f).astype(jnp.bfloat16)
    pad_first = with_rims(act_first)
    hidden_first = rounded(convolve(pad_first, conv_first))
    act_second = jax.nn.silu(hidden_first.astype(jnp.float32)).astype(jnp.bfloat16)
    pad_second = with_rims(act_second)
    summed = rounded(inputs_f + convolve(pad_second, conv_second))
    summed_f = summed.astype(jnp.float32)
    centred = summed_f - jnp.mean(summed_f, axis=-1, keepdims=True)
    inv_scale = lax.rsqrt(jnp.mean(centred * centred, axis=-1, keepdims=True) + 1e-05)
    normed_f = centred * inv_scale
    normed = normed_f.astype(jnp.bfloat16)
    flat_normed = normed.reshape(pixels, chan)
    flat_cot = cotangent.reshape(pixels, chan)
    grad_mixed = project_back(flat_cot, w_out).astype(jnp.bfloat16)

    def to_pixels(array):
        return array.reshape(1, views, share, chan)

    def pixel_items(array):
        return array.reshape(views, share, chan)

    def to_views(array):
        return array.reshape(views, 1, share, chan)

    arrived = (
        lax.all_to_all(to_pixels(flat_normed), "view", split_axis=1, concat_axis=0, tiled=True),
        lax.all_to_all(to_pixels(grad_mixed), "view", split_axis=1, concat_axis=0, tiled=True),
    )
    normed_pix = pixel_items(arrived[0])
    grad_pix = pixel_items(arrived[1])
    rows_pix = normed_pix.reshape(-1, chan)
    query = project(rows_pix, w_query).reshape(views, share, chan)
    key = project(rows_pix, w_key).reshape(views, share, chan)
    value = project(rows_pix, w_value).reshape(views, share, chan)
    mixed, grad_query, grad_key, grad_value = attend(query, key, value, grad_pix)
    flat_gq = grad_query.reshape(-1, chan)
    flat_gk = grad_key.reshape(-1, chan)
    flat_gv = grad_value.reshape(-1, chan)
    grad_wq = outer_sum(rows_pix, flat_gq)
    grad_wk = outer_sum(rows_pix, flat_gk)
    grad_wv = outer_sum(rows_pix, flat_gv)
    back = (
        project_back(flat_gq, w_query)
        + project_back(flat_gk, w_key)
        + project_back(flat_gv, w_value)
    )
    back = back.astype(jnp.bfloat16).reshape(views, share, chan)
    returned = (
        lax.all_to_all(to_views(mixed), "view", split_axis=0, concat_axis=1, tiled=True),
        lax.all_to_all(to_views(back), "view", split_axis=0, concat_axis=1, tiled=True),
    )
    mixed_rows = returned[0].reshape(pixels, chan)
    grad_normed = returned[1].astype(jnp.float32).reshape(features.shape)
    grad_wo = outer_sum(mixed_rows, flat_cot)
    grad_summed = cotangent.astype(jnp.float32) + inv_scale * (
        grad_normed
        - jnp.mean(grad_normed, axis=-1, keepdims=True)
        - normed_f * jnp.mean(grad_normed * normed_f, axis=-1, keepdims=True)
    )
    grad_second = grad_summed.astype(jnp.bfloat16)
    slope_second = convolve(with_rims(grad_second), flipped(conv_second))
    grad_first = (slope_second * silu_slope(hidden_first.astype(jnp.float32))).astype(jnp.bfloat16)
    slope_first = convolve(with_rims(grad_first), flipped(conv_first))
    grad_features = (grad_summed + slope_first * silu_slope(inputs_f)).astype(jnp.bfloat16)
    conv_part = jnp.stack(
        [kernel_grad(pad_first, grad_first), kernel_grad(pad_second, grad_second)]
    )
    attn_part = jnp.stack([grad_wq, grad_wk, grad_wv, grad_wo])
    whole = (
        lax.psum(conv_part.astype(jnp.bfloat16), "strip").astype(jnp.float32),
        lax.psum(attn_part.astype(jnp.bfloat16), "strip").astype(jnp.float32),
    )
    conv_total, attn_total = (
        lax.psum_scatter(
            whole[0].astype(jnp.bfloat16), "view", scatter_dimension=1, tiled=True
        ).astype(jnp.float32),
        lax.psum_scatter(
            whole[1].astype(jnp.bfloat16), "view", scatter_dimension=1, tiled=True
        ).astype(jnp.float32),
    )
    return (grad_features, conv_total, attn_total)


def solution(mesh):
    return jax.shard_map(
        body,
        mesh=mesh,
        in_specs=(
            P(("orbit", "view"), "strip", None, None),
            P(("orbit", "view"), "strip", None, None),
            P(),
            P(),
            P(),
            P(),
            P(),
            P(),
        ),
        out_specs=(
            P(("orbit", "view"), "strip", None, None),
            P("orbit", "view", None),
            P("orbit", "view", None),
        ),
        check_vma=False,
    )
```

profile of v0, /device:TPU:0, one launch (start us, length us, event | category | flops | bytes accessed | tf_op | source)
XLA Modules:
  0.0 246.5 jit_solution(17187515369203246821)
XLA Ops:
  8.5 4.9 %collective-permute-start = (bf16[1,1,128,256]{2,3,1,0:T(8,128)(2,1)S(1)}, bf16[1,1,128,256]{2,3,1,0:T(8,128)(2,1)S(1)}, u32[]{:S(2)}, u32[]{:S(2)}) collective-permute-start(bf16[1,1,128,256]{2,3,1,0:T(8,128)(2,1)S(1)} %get-tuple-element.52), channel_id=1, source_target_pairs={{0,2},{1,3},{4,6},{5,7},{8,10},{9,11},{12,14},{13,15},{16,18},{17,... | collective-permute-start | bytes 196616 | tf_op jit(solution)/shard_map/ppermute | solution.py:12
  13.4 1.3 collective-permute-start.1
  15.6 4.0 %collective-permute-done.1 = bf16[1,1,128,256]{2,3,1,0:T(8,128)(2,1)S(1)} collective-permute-done((bf16[1,1,128,256]{2,3,1,0:T(8,128)(2,1)S(1)}, bf16[1,1,128,256]{2,3,1,0:T(8,128)(2,1)S(1)}, u32[]{:S(2)}, u32[]{:S(2)}) %collective-permute-start.1) | collective-permute-done | bytes 65568 | tf_op jit(solution)/shard_map/ppermute | solution.py:15
  24.5 1.9 copy.129
  35.6 1.6 collective-permute-start.2
  37.2 1.3 collective-permute-start.3
  39.3 4.0 %collective-permute-done.3 = bf16[1,1,128,256]{2,3,1,0:T(8,128)(2,1)S(1)} collective-permute-done((bf16[1,1,128,256]{2,3,1,0:T(8,128)(2,1)S(1)}, bf16[1,1,128,256]{2,3,1,0:T(8,128)(2,1)S(1)}, u32[]{:S(2)}, u32[]{:S(2)}) %collective-permute-start.3) | collective-permute-done | bytes 65568 | tf_op jit(solution)/shard_map/ppermute | solution.py:15
  44.6 1.4 fusion.223
  47.1 1.8 copy.136
  48.9 1.8 copy.137
  50.7 1.8 copy.139
  52.5 1.8 copy.140
  63.7 4.9 %all-to-all-start = ((bf16[1,8,64,256]{3,2,0,1:T(8,128)(2,1)}), bf16[1,8,64,256]{3,2,0,1:T(8,128)(2,1)S(1)}, u32[]{:S(2)}, u32[]{:S(2)}) async-start(bf16[1,8,64,256]{3,2,0,1:T(8,128)(2,1)} %bitcast.39), calls=%async_computation | async-start | bytes 524288 | tf_op jit(solution)/shard_map/all_to_all | solution.py:147
  69.5 2.4 reverse_bitcast_fusion.1
  72.9 5.4 %all-to-all-done = bf16[1,8,64,256]{3,2,0,1:T(8,128)(2,1)S(1)} async-done(((bf16[1,8,64,256]{3,2,0,1:T(8,128)(2,1)}), bf16[1,8,64,256]{3,2,0,1:T(8,128)(2,1)S(1)}, u32[]{:S(2)}, u32[]{:S(2)}) %all-to-all-start) | async-done | bytes 262176 | tf_op jit(solution)/shard_map/all_to_all | solution.py:147
  78.3 3.4 %all-to-all-start.1 = ((bf16[1,8,64,256]{3,2,0,1:T(8,128)(2,1)}), bf16[1,8,64,256]{3,2,0,1:T(8,128)(2,1)S(1)}, u32[]{:S(2)}, u32[]{:S(2)}) async-start(bf16[1,8,64,256]{3,2,0,1:T(8,128)(2,1)} %bitcast.592), calls=%async_computation.1 | async-start | bytes 524288 | tf_op jit(solution)/shard_map/all_to_all | solution.py:148
  83.9 2.9 %fusion.229 = (f32[64,8]{1,0:T(8,128)}, f32[64,8,8]{1,2,0:T(8,128)}) fusion(bf16[8,64,256]{2,1,0:T(8,128)(2,1)} %bitcast.627, bf16[8,64,256]{2,1,0:T(8,128)(2,1)} %bitcast.629), kind=kOutput, calls=%fused_computation.344 | convolution fusion | flops 2109447 | bytes 542720 | tf_op jit(solution)/shard_map/sub | solution.py:79
  86.7 4.6 %all-to-all-done.1 = bf16[1,8,64,256]{3,2,0,1:T(8,128)(2,1)S(1)} async-done(((bf16[1,8,64,256]{3,2,0,1:T(8,128)(2,1)}), bf16[1,8,64,256]{3,2,0,1:T(8,128)(2,1)S(1)}, u32[]{:S(2)}, u32[]{:S(2)}) %all-to-all-start.1) | async-done | bytes 262176 | tf_op jit(solution)/shard_map/all_to_all | solution.py:148
  92.5 2.4 fusion.7
  94.9 2.5 fusion.6
  100.5 3.6 %all-to-all-start.2 = ((bf16[8,1,64,256]{3,2,1,0:T(8,128)(2,1)}), bf16[8,1,64,256]{3,2,1,0:T(8,128)(2,1)S(1)}, u32[]{:S(2)}, u32[]{:S(2)}) async-start(bf16[8,1,64,256]{3,2,1,0:T(8,128)(2,1)} %bitcast.620), calls=%async_computation.2 | async-start | bytes 524288 | tf_op jit(solution)/shard_map/all_to_all | solution.py:171
  104.1 1.4 fusion.9
  107.7 5.8 %all-to-all-done.2 = bf16[8,1,64,256]{3,2,1,0:T(8,128)(2,1)S(1)} async-done(((bf16[8,1,64,256]{3,2,1,0:T(8,128)(2,1)}), bf16[8,1,64,256]{3,2,1,0:T(8,128)(2,1)S(1)}, u32[]{:S(2)}, u32[]{:S(2)}) %all-to-all-start.2) | async-done | bytes 262176 | tf_op jit(solution)/shard_map/all_to_all | solution.py:171
  113.5 4.0 %all-to-all-start.3 = ((bf16[8,1,64,256]{3,2,1,0:T(8,128)(2,1)}), bf16[8,1,64,256]{3,2,1,0:T(8,128)(2,1)}, u32[]{:S(2)}, u32[]{:S(2)}) async-start(bf16[8,1,64,256]{3,2,1,0:T(8,128)(2,1)} %copy.201), calls=%async_computation.3 | async-start | bytes 524288 | tf_op jit(solution)/shard_map/all_to_all | solution.py:170
  122.8 4.5 %all-to-all-done.3 = bf16[8,1,64,256]{3,2,1,0:T(8,128)(2,1)} async-done(((bf16[8,1,64,256]{3,2,1,0:T(8,128)(2,1)}), bf16[8,1,64,256]{3,2,1,0:T(8,128)(2,1)}, u32[]{:S(2)}, u32[]{:S(2)}) %all-to-all-start.3) | async-done | bytes 262176 | tf_op jit(solution)/shard_map/all_to_all | solution.py:170
  127.3 1.3 fusion.72
  128.6 1.8 pad_maximum_fusion.1
  130.5 1.6 collective-permute-start.4
  132.0 1.3 collective-permute-start.5
  133.3 1.9 fusion.48
  137.1 1.9 fusion.42
  145.5 1.4 fusion.222
  146.8 1.8 copy.161
  148.6 1.8 copy.163
  151.3 1.9 copy.166
  153.2 1.8 copy.167
  155.0 1.8 copy.168
  156.8 1.8 copy.169
  165.0 2.1 copy.170
  171.4 1.6 pad_maximum_fusion
  173.1 4.7 %collective-permute-start.6 = (bf16[1,1,128,256]{2,3,1,0:T(8,128)(2,1)S(1)}, bf16[1,1,128,256]{2,3,1,0:T(8,128)(2,1)S(1)}, u32[]{:S(2)}, u32[]{:S(2)}) collective-permute-start(bf16[1,1,128,256]{2,3,1,0:T(8,128)(2,1)S(1)} %get-tuple-element.40), channel_id=1, source_target_pairs={{0,2},{1,3},{4,6},{5,7},{8,10},{9,11},{12,14},{13,15},{16,18},{17,... | collective-permute-start | bytes 196616 | tf_op jit(solution)/shard_map/ppermute | solution.py:12
  177.7 1.5 collective-permute-start.7
  181.3 2.7 %collective-permute-done.7 = bf16[1,1,128,256]{2,3,1,0:T(8,128)(2,1)S(1)} collective-permute-done((bf16[1,1,128,256]{2,3,1,0:T(8,128)(2,1)S(1)}, bf16[1,1,128,256]{2,3,1,0:T(8,128)(2,1)S(1)}, u32[]{:S(2)}, u32[]{:S(2)}) %collective-permute-start.7) | collective-permute-done | bytes 65568 | tf_op jit(solution)/shard_map/ppermute | solution.py:15
  188.2 1.9 copy.176
  196.2 14.1 %reduce-scatter.3.cloned.1.call-done = bf16[2,288,256]{2,1,0:T(8,128)(2,1)} async-done(((bf16[2,2304,256]{2,1,0:T(8,128)(2,1)}), bf16[2,288,256]{2,1,0:T(8,128)(2,1)}) %reduce-scatter.3.cloned.1.call-update) | async-done | bytes 294928 | tf_op jit(solution)/shard_map/reduce_scatter | solution.py:195
  213.9 22.8 %all-reduce.7.cloned.1.call-done = (bf16[2,288,256]{2,1,0:T(8,128)(2,1)}, bf16[4,32,256]{2,1,0:T(8,128)(2,1)}) async-done(((bf16[2,288,256]{2,1,0:T(8,128)(2,1)}, bf16[4,32,256]{2,1,0:T(8,128)(2,1)}), (bf16[2,288,256]{2,1,0:T(8,128)(2,1)}, bf16[4,32,256]{2,1,0:T(8,128)(2,1)})) %all-reduce.7.cloned.1.call-update) | async-done | bytes 360464 | tf_op jit(solution)/shard_map/psum | solution.py:191
  236.7 1.8 convert_element_type.165
  238.5 1.5 convert_element_type.168
  (260 shorter events, 79.6 us)
Async XLA Ops:
  7.2 75.5 %copy-start = (bf16[256,256]{1,0:T(8,128)(2,1)S(1)}, bf16[256,256]{1,0:T(8,128)(2,1)}, u32[]{:S(2)}) copy-start(bf16[256,256]{1,0:T(8,128)(2,1)} %param.12) | copy-start | bytes 393220
  8.5 7.1 %collective-permute-start = (bf16[1,1,128,256]{2,3,1,0:T(8,128)(2,1)S(1)}, bf16[1,1,128,256]{2,3,1,0:T(8,128)(2,1)S(1)}, u32[]{:S(2)}, u32[]{:S(2)}) collective-permute-start(bf16[1,1,128,256]{2,3,1,0:T(8,128)(2,1)S(1)} %get-tuple-element.52), channel_id=1, source_target_pairs={{0,2},{1,3},{4,6},{5,7},{8,10},{9,11},{12,14},{13,15},{16,18},{17,... | collective-permute-start | bytes 196616 | tf_op jit(solution)/shard_map/ppermute | solution.py:12
  13.4 6.2 %collective-permute-start.1 = (bf16[1,1,128,256]{2,3,1,0:T(8,128)(2,1)S(1)}, bf16[1,1,128,256]{2,3,1,0:T(8,128)(2,1)S(1)}, u32[]{:S(2)}, u32[]{:S(2)}) collective-permute-start(bf16[1,1,128,256]{2,3,1,0:T(8,128)(2,1)S(1)} %get-tuple-element.53), channel_id=1, source_target_pairs={{2,0},{3,1},{6,4},{7,5},{10,8},{11,9},{14,12},{15,13},{18,16},{19,... | collective-permute-start | bytes 196616 | tf_op jit(solution)/shard_map/ppermute | solution.py:15
  21.9 1.8 copy-start.6
  24.5 4.5 %copy-start.1 = (bf16[3,3,256,256]{3,2,1,0:T(8,128)(2,1)S(1)}, bf16[3,3,256,256]{3,2,1,0:T(8,128)(2,1)}, u32[]{:S(2)}) copy-start(bf16[3,3,256,256]{3,2,1,0:T(8,128)(2,1)} %param.10) | copy-start | bytes 3538948
  24.5 4.5 %copy-start.21 = (bf16[1,4,128,256]{3,2,1,0:T(8,128)(2,1)S(1)}, bf16[1,4,128,256]{3,2,1,0:T(8,128)(2,1)}, u32[]{:S(2)}) copy-start(bf16[1,4,128,256]{3,2,1,0:T(8,128)(2,1)} %copy.124) | copy-start | bytes 786436
  29.0 1.5 copy-start.50
  29.2 1.5 copy-start.46
  35.4 3.9 %copy-start.12 = (bf16[1,4,128,256]{2,3,1,0:T(8,128)(2,1)}, bf16[1,4,128,256]{2,3,1,0:T(8,128)(2,1)S(1)}, u32[]{:S(2)}) copy-start(bf16[1,4,128,256]{2,3,1,0:T(8,128)(2,1)S(1)} %copy.133) | copy-start | bytes 786436
  35.6 3.7 %collective-permute-start.2 = (bf16[1,1,128,256]{2,3,1,0:T(8,128)(2,1)S(1)}, bf16[1,1,128,256]{2,3,1,0:T(8,128)(2,1)S(1)}, u32[]{:S(2)}, u32[]{:S(2)}) collective-permute-start(bf16[1,1,128,256]{2,3,1,0:T(8,128)(2,1)S(1)} %get-tuple-element.48), channel_id=1, source_target_pairs={{0,2},{1,3},{4,6},{5,7},{8,10},{9,11},{12,14},{13,15},{16,18},{17,... | collective-permute-start | bytes 196616 | tf_op jit(solution)/shard_map/ppermute | solution.py:12
  37.2 6.2 %collective-permute-start.3 = (bf16[1,1,128,256]{2,3,1,0:T(8,128)(2,1)S(1)}, bf16[1,1,128,256]{2,3,1,0:T(8,128)(2,1)S(1)}, u32[]{:S(2)}, u32[]{:S(2)}) collective-permute-start(bf16[1,1,128,256]{2,3,1,0:T(8,128)(2,1)S(1)} %get-tuple-element.49), channel_id=1, source_target_pairs={{2,0},{3,1},{6,4},{7,5},{10,8},{11,9},{14,12},{15,13},{18,16},{19,... | collective-permute-start | bytes 196616 | tf_op jit(solution)/shard_map/ppermute | solution.py:15
  43.4 10.9 %copy-start.10 = (bf16[1,4,128,256]{2,3,1,0:T(8,128)(2,1)}, bf16[1,4,128,256]{2,3,1,0:T(8,128)(2,1)S(1)}, u32[]{:S(2)}) copy-start(bf16[1,4,128,256]{2,3,1,0:T(8,128)(2,1)S(1)} %get-tuple-element.47) | copy-start | bytes 786436
  43.4 10.9 %copy-start.8 = (bf16[1,4,128,256]{2,3,1,0:T(8,128)(2,1)}, bf16[1,4,128,256]{2,3,1,0:T(8,128)(2,1)S(1)}, u32[]{:S(2)}) copy-start(bf16[1,4,128,256]{2,3,1,0:T(8,128)(2,1)S(1)} %get-tuple-element.46) | copy-start | bytes 786436
  55.3 2.5 %copy-start.3 = (bf16[3,3,256,256]{3,2,1,0:T(8,128)(2,1)S(1)}, bf16[3,3,256,256]{3,2,1,0:T(8,128)(2,1)}, u32[]{:S(2)}) copy-start(bf16[3,3,256,256]{3,2,1,0:T(8,128)(2,1)} %param.11) | copy-start | bytes 3538948
  55.3 2.5 %copy-start.51 = (bf16[1,4,128,256]{3,2,1,0:T(8,128)(2,1)S(1)}, bf16[1,4,128,256]{3,2,1,0:T(8,128)(2,1)}, u32[]{:S(2)}) copy-start(bf16[1,4,128,256]{3,2,1,0:T(8,128)(2,1)} %copy.136) | copy-start | bytes 786436
  56.6 1.5 copy-start.47
  62.6 6.0 %copy-start.11 = (bf16[1,4,128,256]{3,2,1,0:T(8,128)(2,1)S(1)}, bf16[1,4,128,256]{3,2,1,0:T(8,128)(2,1)}, u32[]{:S(2)}) copy-start(bf16[1,4,128,256]{3,2,1,0:T(8,128)(2,1)} %param.9) | copy-start | bytes 786436
  63.7 14.6 %all-to-all-start = ((bf16[1,8,64,256]{3,2,0,1:T(8,128)(2,1)}), bf16[1,8,64,256]{3,2,0,1:T(8,128)(2,1)S(1)}, u32[]{:S(2)}, u32[]{:S(2)}) async-start(bf16[1,8,64,256]{3,2,0,1:T(8,128)(2,1)} %bitcast.39), calls=%async_computation | async-start | bytes 524288 | tf_op jit(solution)/shard_map/all_to_all | solution.py:147
  69.5 2.4 copy-start.56
  71.9 9.8 %copy-start.53 = (bf16[256,256]{1,0:T(8,128)(2,1)S(1)}, bf16[256,256]{1,0:T(8,128)(2,1)}, u32[]{:S(2)}) copy-start(bf16[256,256]{1,0:T(8,128)(2,1)} %param.13) | copy-start | bytes 393220
  71.9 11.7 %copy-start.52 = (bf16[256,256]{1,0:T(8,128)(2,1)S(1)}, bf16[256,256]{1,0:T(8,128)(2,1)}, u32[]{:S(2)}) copy-start(bf16[256,256]{1,0:T(8,128)(2,1)} %param.14) | copy-start | bytes 393220
  78.3 13.1 %all-to-all-start.1 = ((bf16[1,8,64,256]{3,2,0,1:T(8,128)(2,1)}), bf16[1,8,64,256]{3,2,0,1:T(8,128)(2,1)S(1)}, u32[]{:S(2)}, u32[]{:S(2)}) async-start(bf16[1,8,64,256]{3,2,0,1:T(8,128)(2,1)} %bitcast.592), calls=%async_computation.1 | async-start | bytes 524288 | tf_op jit(solution)/shard_map/all_to_all | solution.py:148
  83.9 11.1 %copy-start.20 = (bf16[512,256]{1,0:T(8,128)(2,1)}, bf16[512,256]{1,0:T(8,128)(2,1)S(1)}, u32[]{:S(2)}) copy-start(bf16[512,256]{1,0:T(8,128)(2,1)S(1)} %convolution_convert_fusion.4) | copy-start | bytes 786436
  97.4 1.4 copy-start.55
  99.5 4.6 %copy-start.57 = (f32[64,8]{1,0:T(8,128)S(1)}, f32[64,8]{1,0:T(8,128)}, u32[]{:S(2)}) copy-start(f32[64,8]{1,0:T(8,128)} %get-tuple-element.54) | copy-start | bytes 6148
  100.5 13.1 %all-to-all-start.2 = ((bf16[8,1,64,256]{3,2,1,0:T(8,128)(2,1)}), bf16[8,1,64,256]{3,2,1,0:T(8,128)(2,1)S(1)}, u32[]{:S(2)}, u32[]{:S(2)}) async-start(bf16[8,1,64,256]{3,2,1,0:T(8,128)(2,1)} %bitcast.620), calls=%async_computation.2 | async-start | bytes 524288 | tf_op jit(solution)/shard_map/all_to_all | solution.py:171
  104.1 2.2 copy-start.15
  104.1 2.4 copy-start.17
  113.5 13.8 %all-to-all-start.3 = ((bf16[8,1,64,256]{3,2,1,0:T(8,128)(2,1)}), bf16[8,1,64,256]{3,2,1,0:T(8,128)(2,1)}, u32[]{:S(2)}, u32[]{:S(2)}) async-start(bf16[8,1,64,256]{3,2,1,0:T(8,128)(2,1)} %copy.201), calls=%async_computation.3 | async-start | bytes 524288 | tf_op jit(solution)/shard_map/all_to_all | solution.py:170
  117.6 78.6 %reduce-scatter.5.cloned.1.call-start = ((), (), s32[]{:S(2)}) async-start(), calls=%async_computation.7 | async-start | bytes 589824 | tf_op jit(solution)/shard_map/reduce_scatter | solution.py:198
  130.4 79.9 %reduce-scatter.3.cloned.1.call-start = ((), (), s32[]{:S(2)}) async-start(), calls=%async_computation.6 | async-start | bytes 2654208 | tf_op jit(solution)/shard_map/reduce_scatter | solution.py:195
  130.5 13.1 %collective-permute-start.4 = (bf16[1,1,128,256]{2,3,1,0:T(8,128)(2,1)}, bf16[1,1,128,256]{2,3,1,0:T(8,128)(2,1)S(1)}, u32[]{:S(2)}, u32[]{:S(2)}) collective-permute-start(bf16[1,1,128,256]{2,3,1,0:T(8,128)(2,1)} %get-tuple-element.44), channel_id=1, source_target_pairs={{0,2},{1,3},{4,6},{5,7},{8,10},{9,11},{12,14},{13,15},{16,18},{17,... | collective-permute-start | bytes 196616 | tf_op jit(solution)/shard_map/ppermute | solution.py:12
  132.0 11.5 %collective-permute-start.5 = (bf16[1,1,128,256]{2,3,1,0:T(8,128)(2,1)}, bf16[1,1,128,256]{2,3,1,0:T(8,128)(2,1)S(1)}, u32[]{:S(2)}, u32[]{:S(2)}) collective-permute-start(bf16[1,1,128,256]{2,3,1,0:T(8,128)(2,1)} %get-tuple-element.45), channel_id=1, source_target_pairs={{2,0},{3,1},{6,4},{7,5},{10,8},{11,9},{14,12},{15,13},{18,16},{19,... | collective-permute-start | bytes 196616 | tf_op jit(solution)/shard_map/ppermute | solution.py:15
  139.0 1.9 copy-start.9
  151.3 7.2 %copy-start.4 = (bf16[3,3,256,256]{2,3,1,0:T(8,128)(2,1)S(1)}, bf16[3,3,256,256]{2,3,1,0:T(8,128)(2,1)}, u32[]{:S(2)}) copy-start(bf16[3,3,256,256]{2,3,1,0:T(8,128)(2,1)} %reverse_bitcast_fusion.1) | copy-start | bytes 3538948
  158.5 2.5 %copy-start.48 = (bf16[1,4,128,256]{3,2,1,0:T(8,128)(2,1)S(1)}, bf16[1,4,128,256]{3,2,1,0:T(8,128)(2,1)}, u32[]{:S(2)}) copy-start(bf16[1,4,128,256]{3,2,1,0:T(8,128)(2,1)} %copy.163) | copy-start | bytes 786436
  159.8 1.6 copy-start.44
  165.0 2.1 copy-start.13
  165.0 3.6 %copy-start.7 = (bf16[1,4,128,256]{2,3,1,0:T(8,128)(2,1)S(1)}, bf16[1,4,128,256]{2,3,1,0:T(8,128)(2,1)}, u32[]{:S(2)}) copy-start(bf16[1,4,128,256]{2,3,1,0:T(8,128)(2,1)} %copy-done.6) | copy-start | bytes 786436
  173.0 6.3 %copy-start.2 = (bf16[3,3,256,256]{3,2,1,0:T(8,128)(2,1)S(1)}, bf16[3,3,256,256]{3,2,1,0:T(8,128)(2,1)}, u32[]{:S(2)}) copy-start(bf16[3,3,256,256]{3,2,1,0:T(8,128)(2,1)} %param.10) | copy-start | bytes 3538948
  173.0 63.7 %all-reduce.7.cloned.1.call-start = ((), (), s32[]{:S(2)}) async-start(), calls=%async_computation.8 | async-start | bytes 720896 | tf_op jit(solution)/shard_map/psum | solution.py:191
  173.1 8.2 %collective-permute-start.6 = (bf16[1,1,128,256]{2,3,1,0:T(8,128)(2,1)S(1)}, bf16[1,1,128,256]{2,3,1,0:T(8,128)(2,1)S(1)}, u32[]{:S(2)}, u32[]{:S(2)}) collective-permute-start(bf16[1,1,128,256]{2,3,1,0:T(8,128)(2,1)S(1)} %get-tuple-element.40), channel_id=1, source_target_pairs={{0,2},{1,3},{4,6},{5,7},{8,10},{9,11},{12,14},{13,15},{16,18},{17,... | collective-permute-start | bytes 196616 | tf_op jit(solution)/shard_map/ppermute | solution.py:12
  177.7 6.2 %collective-permute-start.7 = (bf16[1,1,128,256]{2,3,1,0:T(8,128)(2,1)S(1)}, bf16[1,1,128,256]{2,3,1,0:T(8,128)(2,1)S(1)}, u32[]{:S(2)}, u32[]{:S(2)}) collective-permute-start(bf16[1,1,128,256]{2,3,1,0:T(8,128)(2,1)S(1)} %get-tuple-element.41), channel_id=1, source_target_pairs={{2,0},{3,1},{6,4},{7,5},{10,8},{11,9},{14,12},{15,13},{18,16},{19,... | collective-permute-start | bytes 196616 | tf_op jit(solution)/shard_map/ppermute | solution.py:15
  186.4 3.7 %copy-start.23 = (bf16[1,4,128,256]{2,3,1,0:T(8,128)(2,1)S(1)}, bf16[1,4,128,256]{2,3,1,0:T(8,128)(2,1)}, u32[]{:S(2)}) copy-start(bf16[1,4,128,256]{2,3,1,0:T(8,128)(2,1)} %get-tuple-element.15) | copy-start | bytes 786436
  187.4 4.4 %copy-start.22 = (bf16[1,4,128,256]{2,3,1,0:T(8,128)(2,1)S(1)}, bf16[1,4,128,256]{2,3,1,0:T(8,128)(2,1)}, u32[]{:S(2)}) copy-start(bf16[1,4,128,256]{2,3,1,0:T(8,128)(2,1)} %get-tuple-element.14) | copy-start | bytes 786436
  188.2 4.4 %copy-start.5 = (bf16[3,3,256,256]{2,3,1,0:T(8,128)(2,1)S(1)}, bf16[3,3,256,256]{2,3,1,0:T(8,128)(2,1)}, u32[]{:S(2)}) copy-start(bf16[3,3,256,256]{2,3,1,0:T(8,128)(2,1)} %reverse_bitcast_fusion) | copy-start | bytes 3538948
  195.8 14.5 %copy-start.28 = (bf16[1,4,128,256]{3,2,1,0:T(8,128)(2,1)S(1)}, bf16[1,4,128,256]{3,2,1,0:T(8,128)(2,1)}, u32[]{:S(2)}) copy-start(bf16[1,4,128,256]{3,2,1,0:T(8,128)(2,1)} %copy.179) | copy-start | bytes 786436
  210.3 2.3 copy-start.18
  (25 other events, 24.6 us)
Sparse Core Ops, SparseCore 0:
  130.5 29.1 reduce-scatter.4
  173.1 37.1 reduce-scatter.2
  212.7 23.9 all-reduce.6
where the time goes:
time: 249 us; the launch traced here: 247 us
  waiting for transfers between devices  68.1 us (27%)
  local copies, waits for them, and re-layouts  67.7 us (27%)
  matrix products  48.3 us (19%)
  starting transfers between devices  34.1 us (14%)
  between operations  14.8 us (6%)
  other arithmetic  13.5 us (5%)
    slice x36, local copies, waits for them, and re-layouts, convolve(): padded[:, shift_row:shift_row + rows, shift_col:shift_col + cols, :]  42.7 us
    psum x1, waiting for transfers between devices, body(): lax.psum(conv_part.astype(jnp.bfloat16), 'strip').astype(jnp.float32)  22.8 us
    dot_general x36, matrix products, convolve(): jnp.dot(piece, kernel[shift_row, shift_col], preferred_element_type=jnp.f...  16.8 us
    reduce_scatter x1, waiting for transfers between devices, body(): lax.psum_scatter(whole[0].astype(jnp.bfloat16), 'view', scatter_dimension...  14.1 us
    dot_general x18, matrix products, kernel_grad(): lax.dot_general(piece, flat_up, (((0,), (0,)), ((), ())), preferred_eleme...  12.7 us
    ppermute x4, starting transfers between devices, extended(): lax.ppermute(lax.slice_in_dim(block, block.shape[dim] - width, None, axis...  12.7 us
    ppermute x4, waiting for transfers between devices, extended(): lax.ppermute(lax.slice_in_dim(block, 0, width, axis=dim), axis, backward)  10.7 us
    unnamed x119, local copies, waits for them, and re-layouts  8.58 us
  transfers between devices with their start and end apart: 15, of which 9 were waited for; matrix products, arithmetic and copies ran while one was open for 30% of the time, Pallas kernels for 0%

commit v1 on v0

v1 whole, which is shorter than its diff:
```python
import functools

import jax
import jax.numpy as jnp
from jax import lax
from jax.experimental import pallas as pl
from jax.experimental.pallas import tpu as pltpu
from jax.sharding import PartitionSpec as P

MESH = pl.DeviceIdType.MESH
F32 = jnp.float32
BF16 = jnp.bfloat16
NT = (((1,), (1,)), ((), ()))
TN = (((0,), (0,)), ((), ()))


def dot(a, b):
    return jnp.dot(a, b, preferred_element_type=F32)


def dot_nt(a, b):
    return lax.dot_general(a, b, NT, preferred_element_type=F32)


def dot_tn(a, b):
    return lax.dot_general(a, b, TN, preferred_element_type=F32)


def silu(x):
    return x * jax.nn.sigmoid(x)


def silu_slope(x):
    sigma = jax.nn.sigmoid(x)
    return sigma * (1.0 + x * (1.0 - sigma))


def kernel(
    dims, feat, cot, w1, w2, wq, wk, wv, wo, gfeat, conv_out, attn_out,
    cols1, cols2, colsg, halo, hidden, act2, normed, normed_f, inv, g2, g1, gs,
    normp, cotp, backp, gn,
    part_a, part_b, part_c, r1a, r1b, r1c, sum_a, sum_b, sum_c,
    r2a, r2b, r2c, r3a, r3b, r3c,
    halo_send, halo_recv, cot_send, cot_recv, nrm_send, nrm_recv, bck_send, bck_recv,
    s1_send, s1_recv, s2_send, s2_recv, s3_send, s3_recv,
):
    views, strips, rows, width, chan = dims
    pixels = rows * width
    share = pixels // views
    zs = views // 2
    view = lax.axis_index("view")
    strip = lax.axis_index("strip")
    core = lax.rem(view, 2)
    zed = lax.div(view, 2)

    barrier = pltpu.get_barrier_semaphore()
    for k in range(1, views):
        pl.semaphore_signal(
            barrier, inc=1, device_id={"view": lax.rem(view + k, views)}, device_id_type=MESH
        )
    for k in range(1, strips):
        pl.semaphore_signal(
            barrier, inc=1, device_id={"strip": lax.rem(strip + k, strips)}, device_id_type=MESH
        )

    @pl.when(strip == 0)
    def _():
        for e in range(4):
            halo[e, 0] = jnp.zeros((width, chan), BF16)

    @pl.when(strip == strips - 1)
    def _():
        for e in range(4):
            halo[e, 1] = jnp.zeros((width, chan), BF16)

    pl.semaphore_wait(barrier, views - 1 + strips - 1)

    def halo_copies(e, ref):
        up = pltpu.make_async_remote_copy(
            src_ref=ref.at[pl.ds(0, width)], dst_ref=halo.at[e, 1],
            send_sem=halo_send.at[e, 0], recv_sem=halo_recv.at[e, 0],
            device_id={"strip": lax.max(strip - 1, 0)}, device_id_type=MESH,
        )
        down = pltpu.make_async_remote_copy(
            src_ref=ref.at[pl.ds(pixels - width, width)], dst_ref=halo.at[e, 0],
            send_sem=halo_send.at[e, 1], recv_sem=halo_recv.at[e, 1],
            device_id={"strip": lax.min(strip + 1, strips - 1)}, device_id_type=MESH,
        )
        return up, down

    def halo_start(e, ref):
        up, down = halo_copies(e, ref)
        pl.when(strip > 0)(up.start)
        pl.when(strip < strips - 1)(down.start)

    def halo_wait(e, ref):
        up, down = halo_copies(e, ref)

        @pl.when(strip > 0)
        def _():
            up.wait_send()
            down.wait_recv()

        @pl.when(strip < strips - 1)
        def _():
            down.wait_send()
            up.wait_recv()

    def spread(src, dst, send, recv):
        out = []
        for k in range(1, views):
            peer = lax.rem(view + k, views)
            out.append(
                pltpu.make_async_remote_copy(
                    src_ref=src.at[pl.ds(pl.multiple_of(peer * share, share), share)],
                    dst_ref=dst.at[pl.ds(pl.multiple_of(view * share, share), share)],
                    send_sem=send.at[k], recv_sem=recv.at[k],
                    device_id={"view": peer}, device_id_type=MESH,
                )
            )
        return out

    mine = pl.ds(pl.multiple_of(view * share, share), share)

    def start(copies):
        for copy in copies:
            copy.start()

    def wait(copies):
        for copy in copies:
            copy.wait()

    column = lax.rem(lax.broadcasted_iota(jnp.int32, (pixels + 2 * width, chan), 0), width)

    def build(cols, e, centre, act):
        top = act(halo[e, 0].astype(F32))
        low = act(halo[e, 1].astype(F32))
        x = jnp.concatenate([top, centre, low], axis=0)
        count = pixels + 2 * width
        left = jnp.where(column == 0, 0.0, pltpu.roll(x, 1, 0))
        right = jnp.where(column == width - 1, 0.0, pltpu.roll(x, count - 1, 0))
        cols[:, pl.ds(0, chan)] = left.astype(BF16)
        cols[:, pl.ds(chan, chan)] = x.astype(BF16)
        cols[:, pl.ds(2 * chan, chan)] = right.astype(BF16)

    def conv(cols, w):
        total = None
        for r in range(3):
            term = dot(cols[pl.ds(r * width, pixels), :], w[r])
            total = term if total is None else total + term
        return total

    def conv_flip(cols, w):
        total = None
        for r in range(3):
            for s in range(3):
                term = dot_nt(
                    cols[pl.ds(r * width, pixels), pl.ds(s * chan, chan)],
                    w[2 - r, pl.ds((2 - s) * chan, chan), :],
                )
                total = term if total is None else total + term
        return total

    def wgrad(cols, d, out):
        for r in range(3):
            value = dot_tn(cols[pl.ds(r * width, pixels), :], d).astype(BF16)
            flat = out.reshape(9 * chan, chan)
            flat[pl.ds(r * 3 * chan, 3 * chan), :] = value

    def same(x):
        return x

    def stage1(i, part, r1):
        return pltpu.make_async_remote_copy(
            src_ref=part.at[:, 1 - core], dst_ref=r1,
            send_sem=s1_send.at[i], recv_sem=s1_recv.at[i],
            device_id={"view": view + 1 - 2 * core}, device_id_type=MESH,
        )

    def reduce1(part, r1, total):
        for j in range(zs):
            total[j] = (part[j, core].astype(F32) + r1[j].astype(F32)).astype(BF16)

    def stage2(i, total, r2):
        out = []
        for k in range(1, zs):
            other = lax.rem(zed + k, zs)
            out.append(
                pltpu.make_async_remote_copy(
                    src_ref=total.at[other], dst_ref=r2.at[k - 1],
                    send_sem=s2_send.at[i, k], recv_sem=s2_recv.at[i, k],
                    device_id={"view": other * 2 + core}, device_id_type=MESH,
                )
            )
        return out

    def reduce2(total, r2, r3):
        value = total[zed].astype(F32)
        for k in range(1, zs):
            value = value + r2[k - 1].astype(F32)
        r3[strip] = value.astype(BF16)

    def stage3(i, r3):
        out = []
        for k in range(1, strips):
            out.append(
                pltpu.make_async_remote_copy(
                    src_ref=r3.at[strip], dst_ref=r3.at[strip],
                    send_sem=s3_send.at[i, k], recv_sem=s3_recv.at[i, k],
                    device_id={"strip": lax.rem(strip + k, strips)}, device_id_type=MESH,
                )
            )
        return out

    def reduce3(r3):
        value = r3[0].astype(F32)
        for k in range(1, strips):
            value = value + r3[k].astype(F32)
        return value

    halo_start(0, feat)
    cot_copies = spread(cot, cotp, cot_send, cot_recv)
    start(cot_copies)
    cotp[mine, :] = cot[mine, :]
    x = feat[...].astype(F32)
    a1 = silu(x)
    halo_wait(0, feat)
    build(cols1, 0, a1, silu)
    hidden[...] = conv(cols1, w1).astype(BF16)
    act2[...] = silu(hidden[...].astype(F32)).astype(BF16)
    halo_start(1, act2)
    halo_wait(1, act2)
    build(cols2, 1, act2[...].astype(F32), same)
    summed = (feat[...].astype(F32) + conv(cols2, w2)).astype(BF16).astype(F32)
    centred = summed - jnp.mean(summed, axis=-1, keepdims=True)
    scale = lax.rsqrt(jnp.mean(centred * centred, axis=-1, keepdims=True) + 1e-05)
    inv[...] = jnp.broadcast_to(scale, inv.shape)
    nf = centred * scale
    normed_f[...] = nf
    normed[...] = nf.astype(BF16)
    nrm_copies = spread(normed, normp, nrm_send, nrm_recv)
    start(nrm_copies)
    normp[mine, :] = normed[mine, :]
    wait(cot_copies)
    gmix = dot_nt(cotp[...], wo[...]).astype(BF16)
    wait(nrm_copies)

    rp = normp[...]
    query = dot(rp, wq[...]).astype(BF16)
    key = dot(rp, wk[...]).astype(BF16)
    value = dot(rp, wv[...]).astype(BF16)
    n = views * share
    ia = lax.rem(lax.broadcasted_iota(jnp.int32, (n, n), 0), share)
    ib = lax.rem(lax.broadcasted_iota(jnp.int32, (n, n), 1), share)
    factor = chan ** (-0.5)
    scores = jnp.where(ia == ib, dot_nt(query, key) * factor, -jnp.inf)
    expo = jnp.exp(scores - jnp.max(scores, axis=-1, keepdims=True))
    prob_f = expo / jnp.sum(expo, axis=-1, keepdims=True)
    prob = prob_f.astype(BF16)
    mixed = dot(prob, value).astype(BF16)
    grad_prob = dot_nt(gmix, value)
    weighted = prob_f * grad_prob
    inner = jnp.sum(weighted, axis=-1, keepdims=True)
    grad_score = (prob_f * (grad_prob - inner) * factor).astype(BF16)
    grad_value = dot_tn(prob, gmix).astype(BF16)
    grad_query = dot(grad_score, key).astype(BF16)
    grad_key = dot_tn(grad_score, query).astype(BF16)
    back = dot_nt(grad_query, wq[...]) + dot_nt(grad_key, wk[...]) + dot_nt(grad_value, wv[...])
    backp[...] = back.astype(BF16)
    bck_copies = spread(backp, gn, bck_send, bck_recv)
    start(bck_copies)
    gn[mine, :] = backp[mine, :]
    slab = chan // views
    for t, (lhs, rhs) in enumerate(
        ((rp, grad_query), (rp, grad_key), (rp, grad_value), (mixed, cotp[...]))
    ):
        term = dot_tn(lhs, rhs).astype(BF16)
        part_a[:, :, t] = term.reshape(zs, 2, slab, chan)
    a1_copy = stage1(0, part_a, r1a)
    a1_copy.start()

    wait(bck_copies)
    gnf = gn[...].astype(F32)
    nf = normed_f[...]
    gsum = cot[...].astype(F32) + inv[:, 0:1] * (
        gnf
        - jnp.mean(gnf, axis=-1, keepdims=True)
        - nf * jnp.mean(gnf * nf, axis=-1, keepdims=True)
    )
    gs[...] = gsum
    g2[...] = gsum.astype(BF16)
    halo_start(2, g2)
    wgrad(cols2, g2[...], part_b)
    b1_copy = stage1(1, part_b, r1b)
    b1_copy.start()
    a1_copy.wait()
    reduce1(part_a, r1a, sum_a)
    a2_copies = stage2(0, sum_a, r2a)
    start(a2_copies)
    halo_wait(2, g2)
    build(colsg, 2, g2[...].astype(F32), same)
    slope = conv_flip(colsg, w2)
    g1[...] = (slope * silu_slope(hidden[...].astype(F32))).astype(BF16)
    halo_start(3, g1)
    b1_copy.wait()
    reduce1(part_b, r1b, sum_b)
    b2_copies = stage2(1, sum_b, r2b)
    start(b2_copies)
    wgrad(cols1, g1[...], part_c)
    c1_copy = stage1(2, part_c, r1c)
    c1_copy.start()
    halo_wait(3, g1)
    build(colsg, 3, g1[...].astype(F32), same)
    c1_copy.wait()
    reduce1(part_c, r1c, sum_c)
    c2_copies = stage2(2, sum_c, r2c)
    start(c2_copies)
    slope = conv_flip(colsg, w1)
    gfeat[...] = (gs[...] + slope * silu_slope(feat[...].astype(F32))).astype(BF16)
    wait(a2_copies)
    reduce2(sum_a, r2a, r3a)
    a3_copies = stage3(0, r3a)
    start(a3_copies)
    wait(b2_copies)
    reduce2(sum_b, r2b, r3b)
    b3_copies = stage3(1, r3b)
    start(b3_copies)
    wait(a3_copies)
    attn_out[...] = reduce3(r3a)
    wait(b3_copies)
    conv_out[1] = reduce3(r3b)
    wait(c2_copies)
    reduce2(sum_c, r2c, r3c)
    c3_copies = stage3(2, r3c)
    start(c3_copies)
    wait(c3_copies)
    conv_out[0] = reduce3(r3c)


def body(features, cotangent, conv_first, conv_second, w_query, w_key, w_value, w_out):
    views = lax.axis_size("view")
    strips = lax.axis_size("strip")
    _, rows, width, chan = features.shape
    pixels = rows * width
    zs = views // 2
    cut = 9 * chan // views
    slab = chan // views
    vm = pltpu.VMEM
    dma = pltpu.SemaphoreType.DMA
    padded = pixels + 2 * width
    flat = (pixels, chan)
    conv_s = (cut, chan)
    attn_s = (4, slab, chan)
    scratch = [
        vm((padded, 3 * chan), BF16), vm((padded, 3 * chan), BF16), vm((padded, 3 * chan), BF16),
        vm((4, 2, width, chan), BF16),
        vm(flat, BF16), vm(flat, BF16), vm(flat, BF16), vm(flat, F32), vm((pixels, 128), F32),
        vm(flat, BF16), vm(flat, BF16), vm(flat, F32),
        vm(flat, BF16), vm(flat, BF16), vm(flat, BF16), vm(flat, BF16),
        vm((zs, 2) + attn_s, BF16), vm((zs, 2) + conv_s, BF16), vm((zs, 2) + conv_s, BF16),
        vm((zs,) + attn_s, BF16), vm((zs,) + conv_s, BF16), vm((zs,) + conv_s, BF16),
        vm((zs,) + attn_s, BF16), vm((zs,) + conv_s, BF16), vm((zs,) + conv_s, BF16),
        vm((zs - 1,) + attn_s, BF16), vm((zs - 1,) + conv_s, BF16), vm((zs - 1,) + conv_s, BF16),
        vm((strips,) + attn_s, BF16), vm((strips,) + conv_s, BF16), vm((strips,) + conv_s, BF16),
        dma((4, 2)), dma((4, 2)),
        dma((views,)), dma((views,)), dma((views,)), dma((views,)), dma((views,)), dma((views,)),
        dma((3,)), dma((3,)), dma((3, zs)), dma((3, zs)), dma((3, strips)), dma((3, strips)),
    ]
    spec = pl.BlockSpec(memory_space=pltpu.VMEM)
    outs = pl.pallas_call(
        functools.partial(kernel, (views, strips, rows, width, chan)),
        out_shape=(
            jax.ShapeDtypeStruct(flat, BF16),
            jax.ShapeDtypeStruct((2,) + conv_s, F32),
            jax.ShapeDtypeStruct(attn_s, F32),
        ),
        in_specs=[spec] * 8,
        out_specs=(spec, spec, spec),
        scratch_shapes=scratch,
        compiler_params=pltpu.CompilerParams(
            collective_id=0, has_side_effects=True, vmem_limit_bytes=60 * 1024 * 1024
        ),
    )(
        features.reshape(flat),
        cotangent.reshape(flat),
        conv_first.reshape(3, 3 * chan, chan),
        conv_second.reshape(3, 3 * chan, chan),
        w_query, w_key, w_value, w_out,
    )
    return (outs[0].reshape(features.shape), outs[1], outs[2])


def solution(mesh):
    rows = P(("orbit", "view"), "strip", None, None)
    grads = P("orbit", "view", None)
    return jax.shard_map(
        body,
        mesh=mesh,
        in_specs=(rows, rows, P(), P(), P(), P(), P(), P()),
        out_specs=(rows, grads, grads),
        check_vma=False,
    )
```

time: 249 us -> 75.5 us (0.30)
  Pallas kernels: 0 us -> 69.8 us
  waiting for transfers between devices: 68.1 us -> 0 us
  local copies, waits for them, and re-layouts: 67.7 us -> 4.28 us
  matrix products: 48.3 us -> 0 us
  starting transfers between devices: 34.1 us -> 0 us
  between operations: 14.8 us -> 0.65 us
  other arithmetic: 13.5 us -> 0 us
    pallas_call x0 -> x1, Pallas kernels: none -> 69.8 us  [body(): pl.pallas_call(functools.partial(kernel, (views, strips, rows, width, cha...]
    dot_general x70 -> x0, matrix products: 45.5 us -> none  [the longest x36 16.8 us: convolve(): jnp.dot(piece, kernel[shift_row, shift_col], preferred_element_type=jnp.f...]
    slice x40 -> x0, local copies, waits for them, and re-layouts: 43.4 us -> none  [the longest x36 42.7 us: convolve(): padded[:, shift_row:shift_row + rows, shift_col:shift_col + cols, :]]
    psum x1 -> x0, waiting for transfers between devices: 22.8 us -> none  [body(): lax.psum(conv_part.astype(jnp.bfloat16), 'strip').astype(jnp.float32)]
    all_to_all x4 -> x0, waiting for transfers between devices: 20.4 us -> none  [the longest x1 5.79 us: body(): lax.all_to_all(to_views(back), 'view', split_axis=0, concat_axis=1, tiled...]
    ppermute x8 -> x0, starting transfers between devices: 18.1 us -> none  [the longest x4 12.7 us: extended(): lax.ppermute(lax.slice_in_dim(block, block.shape[dim] - width, None, axis...]
    all_to_all x4 -> x0, starting transfers between devices: 15.9 us -> none  [the longest x1 4.88 us: body(): lax.all_to_all(to_pixels(flat_normed), 'view', split_axis=1, concat_axis=...]
    reduce_scatter x2 -> x0, waiting for transfers between devices: 14.1 us -> none  [the longest x1 14.1 us: body(): lax.psum_scatter(whole[0].astype(jnp.bfloat16), 'view', scatter_dimension...]
  transfers between devices with their start and end apart: 15 -> 0, of which waited for: 9 -> 0; matrix products, arithmetic and copies ran while one was open for 30% -> 0% of each run, Pallas kernels for 0% -> 0%
where the time goes in v1:
time: 75.5 us; the launch traced here: 74.7 us
  Pallas kernels  69.8 us (92%)
  local copies, waits for them, and re-layouts  4.28 us (6%)
    pallas_call x1, Pallas kernels, body(): pl.pallas_call(functools.partial(kernel, (views, strips, rows, width, cha...  69.8 us
    unnamed x5, local copies, waits for them, and re-layouts  4.28 us

profile of v1, /device:TPU:0, one launch (start us, length us, event | category | flops | bytes accessed | tf_op | source)
XLA Modules:
  0.0 74.7 jit_solution(11025808613435569982)
XLA Ops:
  0.6 69.8 %shard_map.103 = (bf16[512,256]{1,0:T(8,128)(2,1)}, f32[2,288,256]{2,1,0:T(8,128)}, f32[4,32,256]{2,1,0:T(8,128)}) custom-call(bf16[512,256]{1,0:T(8,128)(2,1)} %bitcast.8, bf16[512,256]{1,0:T(8,128)(2,1)} %bitcast.9, bf16[3,768,256]{2,1,0:T(8,128)(2,1)} %bitcast.5, bf16[3,768,256]{2,1,0:T(8,128)(2,1)} %bitcast.6, bf16[256,256]{1,0:T(8,128)(2,1)} %wq.1, ...), custom_call_target="tpu_custom_call" | custom-call | tf_op jit(solution)/shard_map/pallas_call | solution.py:370
  70.4 0.0 copy-start
  70.4 1.7 %copy.14 = bf16[1,4,128,256]{3,2,1,0:T(8,128)(2,1)} copy(bf16[1,4,128,256]{3,2,1,0:T(8,128)(2,1)} %bitcast.7) | data formatting | bytes 524288
  72.1 1.9 %copy.15 = f32[2,288,256]{2,1,0:T(8,128)} copy(f32[2,288,256]{2,1,0:T(8,128)} %get-tuple-element.13) | data formatting | bytes 1179648
  74.0 0.0 copy-done
  74.0 0.7 copy.16
Async XLA Ops:
  70.4 3.6 %copy-start = (f32[4,32,256]{2,1,0:T(8,128)S(1)}, f32[4,32,256]{2,1,0:T(8,128)}, u32[]{:S(2)}) copy-start(f32[4,32,256]{2,1,0:T(8,128)} %get-tuple-element.14) | copy-start | bytes 393220

commit v2 on v1

--- a/solution.py
+++ b/solution.py
@@ -36,13 +36,14 @@
 
 
 def kernel(
-    dims, feat, cot, w1, w2, wq, wk, wv, wo, gfeat, conv_out, attn_out,
+    dims, feat, cot, w1h, w2h, wqh, wkh, wvh, woh, gfeat, conv_out, attn_out,
+    w1, w2, wq, wk, wv, wo, load,
     cols1, cols2, colsg, halo, hidden, act2, normed, normed_f, inv, g2, g1, gs,
     normp, cotp, backp, gn,
-    part_a, part_b, part_c, r1a, r1b, r1c, sum_a, sum_b, sum_c,
-    r2a, r2b, r2c, r3a, r3b, r3c,
+    part_a, part_b, part_c, r1a, r1b, r1c, t1a, t1b, t1c, r2a, r2b, r2c,
+    t2a, t2b, t2c, r3a, r3b, r3c, r4a, r4b, r4c,
     halo_send, halo_recv, cot_send, cot_recv, nrm_send, nrm_recv, bck_send, bck_recv,
-    s1_send, s1_recv, s2_send, s2_recv, s3_send, s3_recv,
+    s1_send, s1_recv, s2_send, s2_recv, s3_send, s3_recv, s4_send, s4_recv,
 ):
     views, strips, rows, width, chan = dims
     pixels = rows * width
@@ -53,6 +54,14 @@
     core = lax.rem(view, 2)
     zed = lax.div(view, 2)
 
+    loads = [
+        pltpu.make_async_copy(src, dst, load.at[i])
+        for i, (src, dst) in enumerate(
+            ((w1h, w1), (w2h, w2), (woh, wo), (wqh, wq), (wkh, wk), (wvh, wv))
+        )
+    ]
+    for item in loads:
+        item.start()
     barrier = pltpu.get_barrier_semaphore()
     for k in range(1, views):
         pl.semaphore_signal(
@@ -162,61 +171,127 @@
         return total
 
     def wgrad(cols, d, out):
+        pieces, _, _, parts, unit, _ = out.shape
+        per = 3 * chan // unit
         for r in range(3):
             value = dot_tn(cols[pl.ds(r * width, pixels), :], d).astype(BF16)
-            flat = out.reshape(9 * chan, chan)
-            flat[pl.ds(r * 3 * chan, 3 * chan), :] = value
+            for m in range(per):
+                u = r * per + m
+                v, rest = divmod(u, pieces * parts)
+                p, t = divmod(rest, parts)
+                out[p, v // 2, v % 2, t] = value[m * unit : (m + 1) * unit]
 
     def same(x):
         return x
 
-    def stage1(i, part, r1):
-        return pltpu.make_async_remote_copy(
-            src_ref=part.at[:, 1 - core], dst_ref=r1,
-            send_sem=s1_send.at[i], recv_sem=s1_recv.at[i],
-            device_id={"view": view + 1 - 2 * core}, device_id_type=MESH,
-        )
-
-    def reduce1(part, r1, total):
-        for j in range(zs):
-            total[j] = (part[j, core].astype(F32) + r1[j].astype(F32)).astype(BF16)
-
-    def stage2(i, total, r2):
-        out = []
-        for k in range(1, zs):
-            other = lax.rem(zed + k, zs)
-            out.append(
+    def group(base, part, r1, t1, r2, t2, r3, r4):
+        parts = part.shape[3]
+
+        def stage1(p):
+            return [
                 pltpu.make_async_remote_copy(
-                    src_ref=total.at[other], dst_ref=r2.at[k - 1],
-                    send_sem=s2_send.at[i, k], recv_sem=s2_recv.at[i, k],
-                    device_id={"view": other * 2 + core}, device_id_type=MESH,
+                    src_ref=part.at[p, :, 1 - core], dst_ref=r1.at[p],
+                    send_sem=s1_send.at[base + p], recv_sem=s1_recv.at[base + p],
+                    device_id={"view": view + 1 - 2 * core}, device_id_type=MESH,
                 )
-            )
-        return out
-
-    def reduce2(total, r2, r3):
-        value = total[zed].astype(F32)
-        for k in range(1, zs):
-            value = value + r2[k - 1].astype(F32)
-        r3[strip] = value.astype(BF16)
-
-    def stage3(i, r3):
-        out = []
-        for k in range(1, strips):
-            out.append(
-                pltpu.make_async_remote_copy(
-                    src_ref=r3.at[strip], dst_ref=r3.at[strip],
-                    send_sem=s3_send.at[i, k], recv_sem=s3_recv.at[i, k],
-                    device_id={"strip": lax.rem(strip + k, strips)}, device_id_type=MESH,
+            ]
+
+        def reduce1(p):
+            for j in range(zs):
+                for t in range(parts):
+                    t1[p, t, j] = (
+                        part[p, j, core, t].astype(F32) + r1[p, j, t].astype(F32)
+                    ).astype(BF16)
+
+        def stage2(p):
+            out = []
+            for k in range(1, parts):
+                other = lax.rem(strip + k, strips)
+                out.append(
+                    pltpu.make_async_remote_copy(
+                        src_ref=t1.at[p, other], dst_ref=r2.at[p, k - 1],
+                        send_sem=s2_send.at[base + p, k], recv_sem=s2_recv.at[base + p, k],
+                        device_id={"strip": other}, device_id_type=MESH,
+                    )
                 )
-            )
-        return out
-
-    def reduce3(r3):
-        value = r3[0].astype(F32)
-        for k in range(1, strips):
-            value = value + r3[k].astype(F32)
-        return value
+            return out
+
+        def reduce2(p):
+            own = strip if parts > 1 else 0
+            for j in range(zs):
+                value = t1[p, own, j].astype(F32)
+                for k in range(1, parts):
+                    value = value + r2[p, k - 1, j].astype(F32)
+                t2[p, j] = value.astype(BF16)
+
+        def stage3(p):
+            out = []
+            for k in range(1, zs):
+                other = lax.rem(zed + k, zs)
+                out.append(
+                    pltpu.make_async_remote_copy(
+                        src_ref=t2.at[p, other], dst_ref=r3.at[p, k - 1],
+                        send_sem=s3_send.at[base + p, k], recv_sem=s3_recv.at[base + p, k],
+                        device_id={"view": other * 2 + core}, device_id_type=MESH,
+                    )
+                )
+            return out
+
+        def reduce3(p):
+            value = t2[p, zed].astype(F32)
+            for k in range(1, zs):
+                value = value + r3[p, k - 1].astype(F32)
+            r4[p, strip] = value.astype(BF16)
+
+        def stage4(p):
+            out = []
+            for k in range(1, strips):
+                out.append(
+                    pltpu.make_async_remote_copy(
+                        src_ref=r4.at[p, strip], dst_ref=r4.at[p, strip],
+                        send_sem=s4_send.at[base + p, k], recv_sem=s4_recv.at[base + p, k],
+                        device_id={"strip": lax.rem(strip + k, strips)}, device_id_type=MESH,
+                    )
+                )
+            return out
+
+        def final(p):
+            if parts > 1:
+                return [r4[p, t].astype(F32) for t in range(parts)]
+            value = r4[p, 0].astype(F32)
+            for t in range(1, strips):
+                value = value + r4[p, t].astype(F32)
+            return [value]
+
+        reduces = (None, reduce1, reduce2, reduce3)
+        stages = (stage1, stage2, stage3, stage4)
+
+        def launch():
+            for p in range(part.shape[0]):
+                start(stage1(p))
+
+        def advance(k, p):
+            wait(stages[k - 1](p))
+            reduces[k](p)
+            start(stages[k](p))
+
+        def advance_all(k):
+            for p in range(part.shape[0]):
+                advance(k, p)
+
+        def finish(store):
+            for p in range(part.shape[0]):
+                wait(stage4(p))
+                for t, value in enumerate(final(p)):
+                    store(p * parts + t, value)
+
+        return launch, advance_all, finish
+
+    count_a = part_a.shape[0]
+    count_b = part_b.shape[0]
+    launch_a, step_a, finish_a = group(0, part_a, r1a, t1a, r2a, t2a, r3a, r4a)
+    launch_b, step_b, finish_b = group(count_a, part_b, r1b, t1b, r2b, t2b, r3b, r4b)
+    launch_c, step_c, finish_c = group(count_a + count_b, part_c, r1c, t1c, r2c, t2c, r3c, r4c)
 
     halo_start(0, feat)
     cot_copies = spread(cot, cotp, cot_send, cot_recv)
@@ -226,11 +301,13 @@
     a1 = silu(x)
     halo_wait(0, feat)
     build(cols1, 0, a1, silu)
+    loads[0].wait()
     hidden[...] = conv(cols1, w1).astype(BF16)
     act2[...] = silu(hidden[...].astype(F32)).astype(BF16)
     halo_start(1, act2)
     halo_wait(1, act2)
     build(cols2, 1, act2[...].astype(F32), same)
+    loads[1].wait()
     summed = (feat[...].astype(F32) + conv(cols2, w2)).astype(BF16).astype(F32)
     centred = summed - jnp.mean(summed, axis=-1, keepdims=True)
     scale = lax.rsqrt(jnp.mean(centred * centred, axis=-1, keepdims=True) + 1e-05)
@@ -242,7 +319,10 @@
     start(nrm_copies)
     normp[mine, :] = normed[mine, :]
     wait(cot_copies)
+    loads[2].wait()
     gmix = dot_nt(cotp[...], wo[...]).astype(BF16)
+    for item in loads[3:]:
+        item.wait()
     wait(nrm_copies)
 
     rp = normp[...]
@@ -270,14 +350,17 @@
     bck_copies = spread(backp, gn, bck_send, bck_recv)
     start(bck_copies)
     gn[mine, :] = backp[mine, :]
-    slab = chan // views
+    parts = part_a.shape[3]
+    unit = chan // (views * parts)
     for t, (lhs, rhs) in enumerate(
         ((rp, grad_query), (rp, grad_key), (rp, grad_value), (mixed, cotp[...]))
     ):
         term = dot_tn(lhs, rhs).astype(BF16)
-        part_a[:, :, t] = term.reshape(zs, 2, slab, chan)
-    a1_copy = stage1(0, part_a, r1a)
-    a1_copy.start()
+        for u in range(views * parts):
+            v, q = divmod(u, parts)
+            part_a[0, v // 2, v % 2, q, t] = term[u * unit : (u + 1) * unit]
+    launch_a()
+    step_a(1)
 
     wait(bck_copies)
     gnf = gn[...].astype(F32)
@@ -291,50 +374,46 @@
     g2[...] = gsum.astype(BF16)
     halo_start(2, g2)
     wgrad(cols2, g2[...], part_b)
-    b1_copy = stage1(1, part_b, r1b)
-    b1_copy.start()
-    a1_copy.wait()
-    reduce1(part_a, r1a, sum_a)
-    a2_copies = stage2(0, sum_a, r2a)
-    start(a2_copies)
+    launch_b()
+    step_a(2)
+    step_b(1)
     halo_wait(2, g2)
     build(colsg, 2, g2[...].astype(F32), same)
     slope = conv_flip(colsg, w2)
     g1[...] = (slope * silu_slope(hidden[...].astype(F32))).astype(BF16)
     halo_start(3, g1)
-    b1_copy.wait()
-    reduce1(part_b, r1b, sum_b)
-    b2_copies = stage2(1, sum_b, r2b)
-    start(b2_copies)
     wgrad(cols1, g1[...], part_c)
-    c1_copy = stage1(2, part_c, r1c)
-    c1_copy.start()
+    launch_c()
+    step_c(1)
+    step_b(2)
     halo_wait(3, g1)
     build(colsg, 3, g1[...].astype(F32), same)
-    c1_copy.wait()
-    reduce1(part_c, r1c, sum_c)
-    c2_copies = stage2(2, sum_c, r2c)
-    start(c2_copies)
     slope = conv_flip(colsg, w1)
     gfeat[...] = (gs[...] + slope * silu_slope(feat[...].astype(F32))).astype(BF16)
-    wait(a2_copies)
-    reduce2(sum_a, r2a, r3a)
-    a3_copies = stage3(0, r3a)
-    start(a3_copies)
-    wait(b2_copies)
-    reduce2(sum_b, r2b, r3b)
-    b3_copies = stage3(1, r3b)
-    start(b3_copies)
-    wait(a3_copies)
-    attn_out[...] = reduce3(r3a)
-    wait(b3_copies)
-    conv_out[1] = reduce3(r3b)
-    wait(c2_copies)
-    reduce2(sum_c, r2c, r3c)
-    c3_copies = stage3(2, r3c)
-    start(c3_copies)
-    wait(c3_copies)
-    conv_out[0] = reduce3(r3c)
+    step_a(3)
+    step_c(2)
+    step_b(3)
+    step_c(3)
+
+    def store_a(u, value):
+        attn_out[:, pl.ds(u * unit, unit), :] = value.astype(attn_out.dtype)
+
+    def store_conv(i):
+        def store(u, value):
+            size = value.shape[0]
+            conv_out[i, pl.ds(u * size, size), :] = value.astype(conv_out.dtype)
+
+        return store
+
+    finish_a(store_a)
+    finish_b(store_conv(1))
+    finish_c(store_conv(0))
+
+
+def widen(a, b, c, x, y, z):
+    x[...] = a[...]
+    y[...] = b[...].astype(F32)
+    z[...] = c[...].astype(F32)
 
 
 def body(features, cotangent, conv_first, conv_second, w_query, w_key, w_value, w_out):
@@ -349,36 +428,55 @@
     dma = pltpu.SemaphoreType.DMA
     padded = pixels + 2 * width
     flat = (pixels, chan)
-    conv_s = (cut, chan)
-    attn_s = (4, slab, chan)
+    exact = cut % (16 * strips) == 0 and slab % (16 * strips) == 0
+    parts = strips if exact else 1
+    pieces = 3 if cut % (48 * parts) == 0 else 1
+    conv_u = (cut // (parts * pieces), chan)
+    attn_u = (4, slab // parts, chan)
+    units = ((1, attn_u), (pieces, conv_u), (pieces, conv_u))
+    total = 1 + 2 * pieces
+    hold = [
+        [(n, zs, 2, parts) + u for n, u in units],
+        [(n, zs, parts) + u for n, u in units],
+        [(n, parts, zs) + u for n, u in units],
+        [(n, max(parts - 1, 1), zs) + u for n, u in units],
+        [(n, zs) + u for n, u in units],
+        [(n, zs - 1) + u for n, u in units],
+        [(n, strips) + u for n, u in units],
+    ]
+    conv_k = (3, 3 * chan, chan)
+    square = (chan, chan)
     scratch = [
+        vm(conv_k, BF16), vm(conv_k, BF16),
+        vm(square, BF16), vm(square, BF16), vm(square, BF16), vm(square, BF16), dma((6,)),
         vm((padded, 3 * chan), BF16), vm((padded, 3 * chan), BF16), vm((padded, 3 * chan), BF16),
         vm((4, 2, width, chan), BF16),
         vm(flat, BF16), vm(flat, BF16), vm(flat, BF16), vm(flat, F32), vm((pixels, 128), F32),
         vm(flat, BF16), vm(flat, BF16), vm(flat, F32),
         vm(flat, BF16), vm(flat, BF16), vm(flat, BF16), vm(flat, BF16),
-        vm((zs, 2) + attn_s, BF16), vm((zs, 2) + conv_s, BF16), vm((zs, 2) + conv_s, BF16),
-        vm((zs,) + attn_s, BF16), vm((zs,) + conv_s, BF16), vm((zs,) + conv_s, BF16),
-        vm((zs,) + attn_s, BF16), vm((zs,) + conv_s, BF16), vm((zs,) + conv_s, BF16),
-        vm((zs - 1,) + attn_s, BF16), vm((zs - 1,) + conv_s, BF16), vm((zs - 1,) + conv_s, BF16),
-        vm((strips,) + attn_s, BF16), vm((strips,) + conv_s, BF16), vm((strips,) + conv_s, BF16),
+        *[vm(shape, BF16) for shapes in hold for shape in shapes],
         dma((4, 2)), dma((4, 2)),
         dma((views,)), dma((views,)), dma((views,)), dma((views,)), dma((views,)), dma((views,)),
-        dma((3,)), dma((3,)), dma((3, zs)), dma((3, zs)), dma((3, strips)), dma((3, strips)),
+        dma((total,)), dma((total,)), dma((total, strips)), dma((total, strips)),
+        dma((total, zs)), dma((total, zs)), dma((total, strips)), dma((total, strips)),
     ]
     spec = pl.BlockSpec(memory_space=pltpu.VMEM)
+    stay = pl.BlockSpec(memory_space=pl.ANY)
+    kind = BF16 if exact else F32
+    conv_s = (2, cut, chan)
+    attn_s = (4, slab, chan)
     outs = pl.pallas_call(
         functools.partial(kernel, (views, strips, rows, width, chan)),
         out_shape=(
             jax.ShapeDtypeStruct(flat, BF16),
-            jax.ShapeDtypeStruct((2,) + conv_s, F32),
-            jax.ShapeDtypeStruct(attn_s, F32),
+            jax.ShapeDtypeStruct(conv_s, kind),
+            jax.ShapeDtypeStruct(attn_s, kind),
         ),
-        in_specs=[spec] * 8,
+        in_specs=[spec] * 2 + [stay] * 6,
         out_specs=(spec, spec, spec),
         scratch_shapes=scratch,
         compiler_params=pltpu.CompilerParams(
-            collective_id=0, has_side_effects=True, vmem_limit_bytes=60 * 1024 * 1024
+            collective_id=0, has_side_effects=True, vmem_limit_bytes=56 * 1024 * 1024
         ),
     )(
         features.reshape(flat),
@@ -387,6 +485,16 @@
         conv_second.reshape(3, 3 * chan, chan),
         w_query, w_key, w_value, w_out,
     )
+    outs = pl.pallas_call(
+        widen,
+        out_shape=(
+            jax.ShapeDtypeStruct(flat, BF16),
+            jax.ShapeDtypeStruct(conv_s, F32),
+            jax.ShapeDtypeStruct(attn_s, F32),
+        ),
+        in_specs=[spec] * 3,
+        out_specs=(spec, spec, spec),
+    )(*outs)
     return (outs[0].reshape(features.shape), outs[1], outs[2])
 
 

time: 75.5 us -> 62.2 us (0.82)
  Pallas kernels: 69.8 us -> 61.4 us
  local copies, waits for them, and re-layouts: 4.28 us -> 0 us
    pallas_call x1, Pallas kernels: 69.8 us -> 59.4 us  [body(): pl.pallas_call(functools.partial(kernel, (views, strips, rows, width, cha...]
    unnamed x5 -> x0, local copies, waits for them, and re-layouts: 4.28 us -> none
    pallas_call x0 -> x1, Pallas kernels: none -> 2.03 us  [body(): pl.pallas_call(widen, out_shape=(jax.ShapeDtypeStruct(flat, BF16), jax.Sh...]
where the time goes in v2:
time: 62.2 us; the launch traced here: 62.1 us
  Pallas kernels  61.4 us (99%)
  between operations  0.64 us (1%)
    pallas_call x1, Pallas kernels, body(): pl.pallas_call(functools.partial(kernel, (views, strips, rows, width, cha...  59.4 us
    pallas_call x1, Pallas kernels, body(): pl.pallas_call(widen, out_shape=(jax.ShapeDtypeStruct(flat, BF16), jax.Sh...  2.03 us

profile of v2, /device:TPU:0, one launch (start us, length us, event | category | flops | bytes accessed | tf_op | source)
XLA Modules:
  0.0 62.1 jit_solution(15664250602164104253)
XLA Ops:
  0.6 59.4 %shard_map.103 = (bf16[512,256]{1,0:T(8,128)(2,1)}, bf16[2,288,256]{2,1,0:T(8,128)(2,1)}, bf16[4,32,256]{2,1,0:T(8,128)(2,1)}) custom-call(bf16[512,256]{1,0:T(8,128)(2,1)} %bitcast.7, bf16[512,256]{1,0:T(8,128)(2,1)} %bitcast.8, bf16[3,768,256]{2,1,0:T(8,128)(2,1)} %bitcast.5, bf16[3,768,256]{2,1,0:T(8,128)(2,1)} %bitcast.6, bf16[256,256]{1,0:T(8,128)(2,1)} %wqh.1, ...), custom_call_target="tpu_custom_call" | custom-call | tf_op jit(solution)/shard_map/pallas_call | solution.py:468
  60.0 2.0 %shard_map.104 = (bf16[512,256]{1,0:T(8,128)(2,1)}, f32[2,288,256]{2,1,0:T(8,128)}, f32[4,32,256]{2,1,0:T(8,128)}) custom-call(bf16[512,256]{1,0:T(8,128)(2,1)} %get-tuple-element.9.a, bf16[2,288,256]{2,1,0:T(8,128)(2,1)} %get-tuple-element.10.b, bf16[4,32,256]{2,1,0:T(8,128)(2,1)} %get-tuple-element.11.c), custom_call_target="tpu_custom_call" | custom-call | tf_op jit(solution)/shard_map/pallas_call | solution.py:488

commit v3 on v2

--- a/solution.py
+++ b/solution.py
@@ -38,7 +38,7 @@
 def kernel(
     dims, feat, cot, w1h, w2h, wqh, wkh, wvh, woh, gfeat, conv_out, attn_out,
     w1, w2, wq, wk, wv, wo, load,
-    cols1, cols2, colsg, halo, hidden, act2, normed, normed_f, inv, g2, g1, gs,
+    cols1, cols2, colsg, halo, hidden, normed, normed_f, inv, g2, gs,
     normp, cotp, backp, gn,
     part_a, part_b, part_c, r1a, r1b, r1c, t1a, t1b, t1c, r2a, r2b, r2c,
     t2a, t2b, t2c, r3a, r3b, r3c, r4a, r4b, r4c,
@@ -74,24 +74,24 @@
 
     @pl.when(strip == 0)
     def _():
-        for e in range(4):
-            halo[e, 0] = jnp.zeros((width, chan), BF16)
+        for e in range(2):
+            halo[e, 0] = jnp.zeros((2 * width, chan), BF16)
 
     @pl.when(strip == strips - 1)
     def _():
-        for e in range(4):
-            halo[e, 1] = jnp.zeros((width, chan), BF16)
+        for e in range(2):
+            halo[e, 1] = jnp.zeros((2 * width, chan), BF16)
 
     pl.semaphore_wait(barrier, views - 1 + strips - 1)
 
     def halo_copies(e, ref):
         up = pltpu.make_async_remote_copy(
-            src_ref=ref.at[pl.ds(0, width)], dst_ref=halo.at[e, 1],
+            src_ref=ref.at[pl.ds(0, 2 * width)], dst_ref=halo.at[e, 1],
             send_sem=halo_send.at[e, 0], recv_sem=halo_recv.at[e, 0],
             device_id={"strip": lax.max(strip - 1, 0)}, device_id_type=MESH,
         )
         down = pltpu.make_async_remote_copy(
-            src_ref=ref.at[pl.ds(pixels - width, width)], dst_ref=halo.at[e, 0],
+            src_ref=ref.at[pl.ds(pixels - 2 * width, 2 * width)], dst_ref=halo.at[e, 0],
             send_sem=halo_send.at[e, 1], recv_sem=halo_recv.at[e, 1],
             device_id={"strip": lax.min(strip + 1, strips - 1)}, device_id_type=MESH,
         )
@@ -139,50 +139,55 @@
         for copy in copies:
             copy.wait()
 
-    column = lax.rem(lax.broadcasted_iota(jnp.int32, (pixels + 2 * width, chan), 0), width)
-
-    def build(cols, e, centre, act):
-        top = act(halo[e, 0].astype(F32))
-        low = act(halo[e, 1].astype(F32))
-        x = jnp.concatenate([top, centre, low], axis=0)
-        count = pixels + 2 * width
+    wide = pixels + 2 * width
+    place = lax.broadcasted_iota(jnp.int32, (wide, chan), 0)
+    above = jnp.where(strip == 0, width, 0)
+    below = jnp.where(strip == strips - 1, wide - width, wide)
+    inside = (place >= above) & (place < below)
+
+    def extend(e, centre):
+        return jnp.concatenate(
+            [halo[e, 0].astype(F32), centre.astype(F32), halo[e, 1].astype(F32)], axis=0
+        )
+
+    def build(cols, x):
+        count = x.shape[0]
+        column = lax.rem(lax.broadcasted_iota(jnp.int32, x.shape, 0), width)
         left = jnp.where(column == 0, 0.0, pltpu.roll(x, 1, 0))
         right = jnp.where(column == width - 1, 0.0, pltpu.roll(x, count - 1, 0))
-        cols[:, pl.ds(0, chan)] = left.astype(BF16)
-        cols[:, pl.ds(chan, chan)] = x.astype(BF16)
-        cols[:, pl.ds(2 * chan, chan)] = right.astype(BF16)
-
-    def conv(cols, w):
+        span = pl.ds(0, count)
+        cols[span, pl.ds(0, chan)] = left.astype(BF16)
+        cols[span, pl.ds(chan, chan)] = x.astype(BF16)
+        cols[span, pl.ds(2 * chan, chan)] = right.astype(BF16)
+
+    def conv(cols, w, count):
         total = None
         for r in range(3):
-            term = dot(cols[pl.ds(r * width, pixels), :], w[r])
+            term = dot(cols[pl.ds(r * width, count), :], w[r])
             total = term if total is None else total + term
         return total
 
-    def conv_flip(cols, w):
+    def conv_flip(cols, w, count):
         total = None
         for r in range(3):
             for s in range(3):
                 term = dot_nt(
-                    cols[pl.ds(r * width, pixels), pl.ds(s * chan, chan)],
+                    cols[pl.ds(r * width, count), pl.ds(s * chan, chan)],
                     w[2 - r, pl.ds((2 - s) * chan, chan), :],
                 )
                 total = term if total is None else total + term
         return total
 
-    def wgrad(cols, d, out):
+    def wgrad(cols, d, out, skip):
         pieces, _, _, parts, unit, _ = out.shape
         per = 3 * chan // unit
         for r in range(3):
-            value = dot_tn(cols[pl.ds(r * width, pixels), :], d).astype(BF16)
+            value = dot_tn(cols[pl.ds(skip + r * width, pixels), :], d).astype(BF16)
             for m in range(per):
                 u = r * per + m
                 v, rest = divmod(u, pieces * parts)
                 p, t = divmod(rest, parts)
                 out[p, v // 2, v % 2, t] = value[m * unit : (m + 1) * unit]
-
-    def same(x):
-        return x
 
     def group(base, part, r1, t1, r2, t2, r3, r4):
         parts = part.shape[3]
@@ -297,18 +302,14 @@
     cot_copies = spread(cot, cotp, cot_send, cot_recv)
     start(cot_copies)
     cotp[mine, :] = cot[mine, :]
-    x = feat[...].astype(F32)
-    a1 = silu(x)
     halo_wait(0, feat)
-    build(cols1, 0, a1, silu)
+    build(cols1, silu(extend(0, feat[...])))
     loads[0].wait()
-    hidden[...] = conv(cols1, w1).astype(BF16)
-    act2[...] = silu(hidden[...].astype(F32)).astype(BF16)
-    halo_start(1, act2)
-    halo_wait(1, act2)
-    build(cols2, 1, act2[...].astype(F32), same)
+    hidden[...] = conv(cols1, w1, wide).astype(BF16)
+    act2 = silu(hidden[...].astype(F32)).astype(BF16).astype(F32)
+    build(cols2, jnp.where(inside, act2, 0.0))
     loads[1].wait()
-    summed = (feat[...].astype(F32) + conv(cols2, w2)).astype(BF16).astype(F32)
+    summed = (feat[...].astype(F32) + conv(cols2, w2, pixels)).astype(BF16).astype(F32)
     centred = summed - jnp.mean(summed, axis=-1, keepdims=True)
     scale = lax.rsqrt(jnp.mean(centred * centred, axis=-1, keepdims=True) + 1e-05)
     inv[...] = jnp.broadcast_to(scale, inv.shape)
@@ -372,23 +373,21 @@
     )
     gs[...] = gsum
     g2[...] = gsum.astype(BF16)
-    halo_start(2, g2)
-    wgrad(cols2, g2[...], part_b)
+    halo_start(1, g2)
+    wgrad(cols2, g2[...], part_b, 0)
     launch_b()
     step_a(2)
     step_b(1)
-    halo_wait(2, g2)
-    build(colsg, 2, g2[...].astype(F32), same)
-    slope = conv_flip(colsg, w2)
-    g1[...] = (slope * silu_slope(hidden[...].astype(F32))).astype(BF16)
-    halo_start(3, g1)
-    wgrad(cols1, g1[...], part_c)
+    halo_wait(1, g2)
+    build(colsg, extend(1, g2[...]))
+    slope = conv_flip(colsg, w2, wide)
+    g1 = (slope * silu_slope(hidden[...].astype(F32))).astype(BF16)
+    wgrad(cols1, g1[width : width + pixels], part_c, width)
     launch_c()
+    build(colsg, jnp.where(inside, g1.astype(F32), 0.0))
     step_c(1)
     step_b(2)
-    halo_wait(3, g1)
-    build(colsg, 3, g1[...].astype(F32), same)
-    slope = conv_flip(colsg, w1)
+    slope = conv_flip(colsg, w1, pixels)
     gfeat[...] = (gs[...] + slope * silu_slope(feat[...].astype(F32))).astype(BF16)
     step_a(3)
     step_c(2)
@@ -427,6 +426,7 @@
     vm = pltpu.VMEM
     dma = pltpu.SemaphoreType.DMA
     padded = pixels + 2 * width
+    far = pixels + 4 * width
     flat = (pixels, chan)
     exact = cut % (16 * strips) == 0 and slab % (16 * strips) == 0
     parts = strips if exact else 1
@@ -449,13 +449,12 @@
     scratch = [
         vm(conv_k, BF16), vm(conv_k, BF16),
         vm(square, BF16), vm(square, BF16), vm(square, BF16), vm(square, BF16), dma((6,)),
-        vm((padded, 3 * chan), BF16), vm((padded, 3 * chan), BF16), vm((padded, 3 * chan), BF16),
-        vm((4, 2, width, chan), BF16),
-        vm(flat, BF16), vm(flat, BF16), vm(flat, BF16), vm(flat, F32), vm((pixels, 128), F32),
-        vm(flat, BF16), vm(flat, BF16), vm(flat, F32),
+        vm((far, 3 * chan), BF16), vm((padded, 3 * chan), BF16), vm((far, 3 * chan), BF16),
+        vm((2, 2, 2 * width, chan), BF16), vm((padded, chan), BF16),
+        vm(flat, BF16), vm(flat, F32), vm((pixels, 128), F32), vm(flat, BF16), vm(flat, F32),
         vm(flat, BF16), vm(flat, BF16), vm(flat, BF16), vm(flat, BF16),
         *[vm(shape, BF16) for shapes in hold for shape in shapes],
-        dma((4, 2)), dma((4, 2)),
+        dma((2, 2)), dma((2, 2)),
         dma((views,)), dma((views,)), dma((views,)), dma((views,)), dma((views,)), dma((views,)),
         dma((total,)), dma((total,)), dma((total, strips)), dma((total, strips)),
         dma((total, zs)), dma((total, zs)), dma((total, strips)), dma((total, strips)),

time: 62.2 us -> 63.7 us (1.024)
  Pallas kernels: 61.4 us -> 62.9 us
    pallas_call x1, Pallas kernels: 59.4 us -> 60.9 us  [body(): pl.pallas_call(functools.partial(kernel, (views, strips, rows, width, cha...]
where the time goes in v3:
time: 63.7 us; the launch traced here: 63.6 us
  Pallas kernels  62.9 us (99%)
  between operations  0.64 us (1%)
    pallas_call x1, Pallas kernels, body(): pl.pallas_call(functools.partial(kernel, (views, strips, rows, width, cha...  60.9 us
    pallas_call x1, Pallas kernels, body(): pl.pallas_call(widen, out_shape=(jax.ShapeDtypeStruct(flat, BF16), jax.Sh...  2.03 us

profile of v3, /device:TPU:0, one launch (start us, length us, event | category | flops | bytes accessed | tf_op | source)
XLA Modules:
  0.0 63.6 jit_solution(15301685986139960464)
XLA Ops:
  0.6 60.9 %shard_map.103 = (bf16[512,256]{1,0:T(8,128)(2,1)}, bf16[2,288,256]{2,1,0:T(8,128)(2,1)}, bf16[4,32,256]{2,1,0:T(8,128)(2,1)}) custom-call(bf16[512,256]{1,0:T(8,128)(2,1)} %bitcast.7, bf16[512,256]{1,0:T(8,128)(2,1)} %bitcast.8, bf16[3,768,256]{2,1,0:T(8,128)(2,1)} %bitcast.5, bf16[3,768,256]{2,1,0:T(8,128)(2,1)} %bitcast.6, bf16[256,256]{1,0:T(8,128)(2,1)} %wqh.1, ...), custom_call_target="tpu_custom_call" | custom-call | tf_op jit(solution)/shard_map/pallas_call | solution.py:467
  61.6 2.0 %shard_map.104 = (bf16[512,256]{1,0:T(8,128)(2,1)}, f32[2,288,256]{2,1,0:T(8,128)}, f32[4,32,256]{2,1,0:T(8,128)}) custom-call(bf16[512,256]{1,0:T(8,128)(2,1)} %get-tuple-element.9.a, bf16[2,288,256]{2,1,0:T(8,128)(2,1)} %get-tuple-element.10.b, bf16[4,32,256]{2,1,0:T(8,128)(2,1)} %get-tuple-element.11.c), custom_call_target="tpu_custom_call" | custom-call | tf_op jit(solution)/shard_map/pallas_call | solution.py:487
